TPU v7x, 32 devices: a whole 2x2x4 slice. The times are simulated.
32 devices in a mesh: groups: 2 (over y), tile: 4 (over z), image: 4 (over x, core).
Axes of the slice: x: 2, y: 2, z: 4, core: 2. Of those that a mesh axis runs over, the one named last changes fastest.
Arguments:
- images: bfloat16 [8, 16, 64, 256], P(('groups', 'image'), 'tile'), parts along dimension 0, may hold values from -12 to 12
- cotangent: bfloat16 [8, 16, 64, 256], P(('groups', 'image'), 'tile'), parts along dimension 0, may hold values from -12 to 12
- timesteps: int32 [8], P(('groups', 'image')), parts along dimension 0, may hold values from 0 to 999
- class_ids: int32 [8], P(('groups', 'image')), parts along dimension 0, may hold values from 0 to 999
- norm_gain: float32 [256], replicated, may hold values from 0.25 to 1.75
- norm_bias: float32 [256], replicated, may hold values from -3 to 3
- conv_first: bfloat16 [3, 3, 256, 256], replicated, may hold values from -0.125 to 0.125
- conv_second: bfloat16 [3, 3, 256, 256], replicated, may hold values from -0.125 to 0.125
- time_weight: bfloat16 [256, 1024], P(None, 'tile'), may hold values from -0.375 to 0.375
- time_bias: float32 [1024], P('tile'), may hold values from -3 to 3
- class_table: bfloat16 [1000, 1024], P(None, 'tile'), may hold values from -5 to 5
- adaptive_weight: bfloat16 [1024, 512], P('tile'), may hold values from -0.1875 to 0.1875
- adaptive_bias: float32 [512], replicated, may hold values from -2 to 2
Outputs:
- branch: bfloat16 [8, 16, 64, 256], P(('groups', 'image'), 'tile'), parts along dimension 0
- input_grad: bfloat16 [8, 16, 64, 256], P(('groups', 'image'), 'tile'), parts along dimension 0
- grad_adaptive_weight: float32 [2048, 512], P(('groups', 'tile')), parts along dimension 0
- grad_adaptive_bias: float32 [1024], P('groups'), parts along dimension 0
There are 2 independent parts, one for each index of `groups`. A program takes and returns all parts, laid end to end along the dimension named above; an argument that names none is the same for every part. Nothing has to cross between parts.
All inputs are finite; a program needn't handle non-finite values.
Results may differ from a plain program's by a relative error of at most 0.013.
Values may be sent and summed in bfloat16 or wider, within the bound.
A program may use at most 64 MiB of HBM per device.

v0:
```python
import math
import jax
import jax.numpy as jnp
from jax import lax
from jax.sharding import PartitionSpec as P

GN_GROUPS = 32
EPSILON = 1e-05


def with_halo(block, sides, width):
    for axis, dim in sides:
        count = lax.axis_size(axis)
        forward = [(i, i + 1) for i in range(count - 1)]
        backward = [(target, source) for source, target in forward]
        low = lax.ppermute(
            lax.slice_in_dim(block, block.shape[dim] - width, None, axis=dim), axis, forward
        )
        high = lax.ppermute(lax.slice_in_dim(block, 0, width, axis=dim), axis, backward)
        block = jnp.concatenate([low, block, high], axis=dim)
    return block


def silu_grad(pre_values):
    sigma = jax.nn.sigmoid(pre_values)
    return sigma * (1.0 + pre_values * (1.0 - sigma))


def conv_rows(padded, kernel):
    row_count = padded.shape[1] - 2
    col_count = padded.shape[2]
    channels = padded.shape[3]
    padded_cols = jnp.pad(padded, ((0, 0), (0, 0), (1, 1), (0, 0)))
    widened = jnp.concatenate(
        [padded_cols[:, :, offset : offset + col_count] for offset in range(3)], axis=3
    )
    summed = None
    for offset in range(3):
        row_block = widened[:, offset : offset + row_count].reshape(-1, 3 * channels)
        product = jnp.dot(
            row_block, kernel[offset].reshape(3 * channels, -1), preferred_element_type=jnp.float32
        )
        summed = product if summed is None else summed + product
    return summed.reshape(padded.shape[0], row_count, col_count, -1)


def group_total(values):
    return values.reshape(values.shape[0], GN_GROUPS, -1).sum(axis=2)


def spread_groups(values, channels):
    return jnp.repeat(values, channels // GN_GROUPS, axis=1)[:, None, None, :]


def cell_total(values):
    return (
        values.shape[1] * values.shape[2] * lax.axis_size("tile") * (values.shape[3] // GN_GROUPS)
    )


def moments(values):
    channels = values.shape[3]
    cell_count = cell_total(values)
    first_sum = group_total(jnp.sum(values, axis=(1, 2)))
    square_sum = group_total(jnp.sum(values * values, axis=(1, 2)))
    first_sum, square_sum = lax.psum((first_sum, square_sum), "tile")
    centre = first_sum / cell_count
    spread = square_sum / cell_count - centre * centre
    centre = spread_groups(centre, channels)
    return (centre, spread_groups(lax.rsqrt(spread + EPSILON), channels))


def with_rims(active):
    return with_halo(active, (("tile", 1),), 1)


def first_rims(active, cotangent):
    padded_first = with_rims(active)
    padded_grad = with_halo(cotangent, (("tile", 1),), 1)
    return (padded_first, padded_grad)


def norm_back_first(grad_norm, normed, inverse):
    channels = grad_norm.shape[3]
    cell_count = cell_total(grad_norm)
    plain_sum = group_total(jnp.sum(grad_norm, axis=(1, 2)))
    paired_sum = group_total(jnp.sum(grad_norm * normed, axis=(1, 2)))
    plain_sum, paired_sum = lax.psum((plain_sum, paired_sum), "tile")
    return inverse * (
        grad_norm
        - spread_groups(plain_sum / cell_count, channels)
        - normed * spread_groups(paired_sum / cell_count, channels)
    )


def body(
    images,
    cotangent,
    timesteps,
    class_ids,
    norm_gain,
    norm_bias,
    conv_first,
    conv_second,
    time_weight,
    time_bias,
    class_table,
    adaptive_weight,
    adaptive_bias,
):
    channels = images.shape[3]
    half_freq = time_weight.shape[0] // 2
    frequencies = jnp.exp(-math.log(10000.0) * jnp.arange(half_freq, dtype=jnp.float32) / half_freq)
    angles = timesteps.astype(jnp.float32)[:, None] * frequencies[None]
    sinusoid = jnp.concatenate([jnp.cos(angles), jnp.sin(angles)], axis=1)
    hidden = (
        jnp.dot(sinusoid, time_weight.astype(jnp.float32), precision=lax.Precision.HIGHEST)
        + time_bias
    )
    onehot = (class_ids[:, None] == jnp.arange(class_table.shape[0], dtype=jnp.int32)[None]).astype(
        jnp.float32
    )
    embedding = jax.nn.silu(hidden) + jnp.dot(
        onehot, class_table.astype(jnp.float32), precision=lax.Precision.HIGHEST
    )
    activated = jax.nn.silu(embedding)
    partial_terms = jnp.dot(
        activated, adaptive_weight.astype(jnp.float32), precision=lax.Precision.HIGHEST
    )
    modulation = lax.psum(partial_terms, "tile") + adaptive_bias
    factor_row = 1.0 + modulation[:, :channels]
    factor = factor_row[:, None, None, :]
    shift_term = modulation[:, channels:][:, None, None, :]
    input_float = images.astype(jnp.float32)
    centre_first, inverse_first = moments(input_float)
    normed_first = (input_float - centre_first) * inverse_first
    pre_first = normed_first * norm_gain + norm_bias
    active_first = jax.nn.silu(pre_first).astype(jnp.bfloat16)
    padded_first, padded_grad = first_rims(active_first, cotangent)
    hidden_first = conv_rows(padded_first, conv_first).astype(jnp.bfloat16)
    hidden_float = hidden_first.astype(jnp.float32)
    centre_second, inverse_second = moments(hidden_float)
    normed_second = (hidden_float - centre_second) * inverse_second
    pre_second = normed_second * factor + shift_term
    active_second = jax.nn.silu(pre_second).astype(jnp.bfloat16)
    padded_second = with_rims(active_second)
    branch = conv_rows(padded_second, conv_second).astype(jnp.bfloat16)
    flipped_second = jnp.flip(conv_second, (0, 1)).transpose(0, 1, 3, 2)
    grad_active = conv_rows(padded_grad, flipped_second)
    grad_pre = grad_active * silu_grad(pre_second)
    scale_sum = jnp.sum(grad_pre * normed_second, axis=(1, 2))
    shift_sum = jnp.sum(grad_pre, axis=(1, 2))
    scale_sum, shift_sum = lax.psum((scale_sum, shift_sum), "tile")
    cell_count = cell_total(grad_pre)
    plain_mean = group_total(shift_sum * factor_row) / cell_count
    paired_mean = group_total(scale_sum * factor_row) / cell_count
    grad_norm = grad_pre * factor
    grad_hidden = (
        inverse_second
        * (
            grad_norm
            - spread_groups(plain_mean, channels)
            - normed_second * spread_groups(paired_mean, channels)
        )
    ).astype(jnp.bfloat16)
    flipped_first = jnp.flip(conv_first, (0, 1)).transpose(0, 1, 3, 2)
    padded_hidden = with_halo(grad_hidden, (("tile", 1),), 1)
    grad_active_first = conv_rows(padded_hidden, flipped_first)
    grad_first = grad_active_first * silu_grad(pre_first) * norm_gain
    input_grad = norm_back_first(grad_first, normed_first, inverse_first).astype(jnp.bfloat16)
    pairs = jnp.concatenate([scale_sum, shift_sum], axis=1)
    local_weight = jnp.dot(activated.T, pairs, precision=lax.Precision.HIGHEST)
    local_bias = jnp.sum(pairs, axis=0)
    grad_weight, grad_bias = (
        lax.psum(local_weight.astype(jnp.bfloat16), "image").astype(jnp.float32),
        lax.psum(local_bias.astype(jnp.bfloat16), "image").astype(jnp.float32),
    )
    return (branch, input_grad, grad_weight, grad_bias)


def solution(mesh):
    return jax.shard_map(
        body,
        mesh=mesh,
        in_specs=(
            P(("groups", "image"), "tile", None, None),
            P(("groups", "image"), "tile", None, None),
            P(("groups", "image")),
            P(("groups", "image")),
            P(),
            P(),
            P(),
            P(),
            P(None, "tile"),
            P("tile"),
            P(None, "tile"),
            P("tile", None),
            P(),
        ),
        out_specs=(
            P(("groups", "image"), "tile", None, None),
            P(("groups", "image"), "tile", None, None),
            P(("groups", "tile"), None),
            P("groups"),
        ),
        check_vma=False,
    )
```

profile of v0, /device:TPU:0, one launch (start us, length us, event | category | flops | bytes accessed | tf_op | source)
XLA Modules:
  0.0 125.2 jit_solution(5303490498117019014)
XLA Ops:
  7.2 1.0 convert_reduce_fusion
  8.4 0.1 reduce_sum.168
  8.5 0.1 reduce_sum.165
  8.6 13.5 %all-reduce.7 = (f32[1,32]{1,0:T(1,128)S(1)}, f32[1,32]{1,0:T(1,128)S(1)}) all-reduce(f32[1,32]{1,0:T(1,128)S(1)} %bitcast.139, f32[1,32]{1,0:T(1,128)S(1)} %bitcast.141), channel_id=1, replica_groups=mesh['groups'=2,'tile'=4,'image'=4] {'tile'}, use_global_device_ids=true, to_apply=%region_5.6 | all-reduce | flops 64 | bytes 512 | tf_op jit(solution)/shard_map/psum | solution.py:66
  22.5 1.0 fusion.15
  23.5 0.6 fusion.55
  24.1 1.3 %collective-permute-start.1 = (bf16[1,1,64,256]{3,2,1,0:T(8,128)(2,1)}, bf16[1,1,64,256]{3,2,1,0:T(8,128)(2,1)S(1)}, u32[]{:S(2)}, u32[]{:S(2)}) collective-permute-start(bf16[1,1,64,256]{3,2,1,0:T(8,128)(2,1)} %get-tuple-element.65), channel_id=1, source_target_pairs={{4,0},{8,4},{12,8},{5,1},{9,5},{13,9},{6,2},{10,6},{14,10},{7,3},{... | collective-permute-start | bytes 98312 | tf_op jit(solution)/shard_map/ppermute | solution.py:19
  25.4 4.5 %collective-permute-start = (bf16[1,1,64,256]{3,2,1,0:T(8,128)(2,1)}, bf16[1,1,64,256]{3,2,1,0:T(8,128)(2,1)S(1)}, u32[]{:S(2)}, u32[]{:S(2)}) collective-permute-start(bf16[1,1,64,256]{3,2,1,0:T(8,128)(2,1)} %get-tuple-element.64), channel_id=1, source_target_pairs={{0,4},{4,8},{8,12},{1,5},{5,9},{9,13},{2,6},{6,10},{10,14},{3,7},{... | collective-permute-start | bytes 98312 | tf_op jit(solution)/shard_map/ppermute | solution.py:16
  30.0 1.4 %fusion.53 = (bf16[1,1,64,256]{3,2,1,0:T(8,128)(2,1)}, bf16[1,1,64,256]{3,2,1,0:T(8,128)(2,1)}) fusion(bf16[1,4,64,256]{3,2,1,0:T(8,128)(2,1)} %param.14), kind=kLoop, calls=%fused_computation.107 | loop fusion | bytes 131072 | tf_op jit(solution)/shard_map/slice | solution.py:19
  31.4 1.9 %collective-permute-start.4 = (bf16[1,1,64,256]{3,2,1,0:T(8,128)(2,1)}, bf16[1,1,64,256]{3,2,1,0:T(8,128)(2,1)S(1)}, u32[]{:S(2)}, u32[]{:S(2)}) collective-permute-start(bf16[1,1,64,256]{3,2,1,0:T(8,128)(2,1)} %get-tuple-element.61), channel_id=1, source_target_pairs={{0,4},{4,8},{8,12},{1,5},{5,9},{9,13},{2,6},{6,10},{10,14},{3,7},{... | collective-permute-start | bytes 98312 | tf_op jit(solution)/shard_map/ppermute | solution.py:16
  33.3 1.4 %collective-permute-start.5 = (bf16[1,1,64,256]{3,2,1,0:T(8,128)(2,1)}, bf16[1,1,64,256]{3,2,1,0:T(8,128)(2,1)S(1)}, u32[]{:S(2)}, u32[]{:S(2)}) collective-permute-start(bf16[1,1,64,256]{3,2,1,0:T(8,128)(2,1)} %get-tuple-element.60), channel_id=1, source_target_pairs={{4,0},{8,4},{12,8},{5,1},{9,5},{13,9},{6,2},{10,6},{14,10},{7,3},{... | collective-permute-start | bytes 98312 | tf_op jit(solution)/shard_map/ppermute | solution.py:19
  34.7 2.4 %copy.17 = bf16[3,3,256,256]{2,3,1,0:T(8,128)(2,1)} copy(bf16[3,3,256,256]{3,2,1,0:T(8,128)(2,1)} %param.20) | data formatting | bytes 2359296 | tf_op args[7]
  37.1 1.0 fusion.43
  38.1 0.6 copy-done.2
  38.7 1.0 fusion.44
  39.7 1.6 %copy.18 = bf16[3,3,256,256]{2,3,1,0:T(8,128)(2,1)} copy(bf16[3,3,256,256]{3,2,1,0:T(8,128)(2,1)S(1)} %copy-done.2) | data formatting | bytes 2359296 | tf_op args[6]
  42.8 1.0 fusion.42
  43.8 0.6 copy-done.4
  44.6 0.2 fusion.57
  44.7 0.6 copy-done.16
  45.3 0.1 fusion.31
  45.6 0.2 fusion.58
  46.0 0.1 fusion.48
  46.1 0.9 copy-done.12
  47.0 0.3 fusion.56
  47.3 0.3 convolution_add_fusion.7
  47.6 0.4 copy-done.10
  48.0 0.3 fusion.39
  48.4 0.1 reduce_sum.174
  48.6 0.1 reduce_sum.171
  48.7 11.0 %all-reduce.6 = (f32[1,512]{1,0:T(1,128)S(1)}, f32[1,32]{1,0:T(1,128)S(1)}, f32[1,32]{1,0:T(1,128)S(1)}) all-reduce(f32[1,512]{1,0:T(1,128)S(1)} %fusion.58, f32[1,32]{1,0:T(1,128)S(1)} %bitcast.134, f32[1,32]{1,0:T(1,128)S(1)} %bitcast.135), channel_id=1, replica_groups=mesh['groups'=2,'tile'=4,'image'=4] {'tile'}, use_global_device_ids=true, to_apply=%region_12.13 | all-reduce | flops 576 | bytes 4608 | tf_op jit(solution)/shard_map/psum | solution.py:130
  60.3 0.1 fusion.46
  60.4 0.9 copy-done.8
  61.3 0.3 fusion.60
  61.6 0.3 convolution_add_fusion.3
  61.8 0.4 copy-done.13
  62.3 0.3 fusion.38
  62.6 8.5 %all-reduce.5 = (f32[1,256]{1,0:T(1,128)S(1)}, f32[1,256]{1,0:T(1,128)S(1)}) all-reduce(f32[1,256]{1,0:T(1,128)S(1)} %bitcast.136, f32[1,256]{1,0:T(1,128)S(1)} %bitcast.137), channel_id=1, replica_groups=mesh['groups'=2,'tile'=4,'image'=4] {'tile'}, use_global_device_ids=true, to_apply=%region_14.15 | all-reduce | flops 512 | bytes 4096 | tf_op jit(solution)/shard_map/psum | solution.py:153
  71.2 0.1 reduce_sum.181
  71.6 0.1 reduce_sum.178
  71.9 0.2 multiply_convert_fusion.1
  72.1 1.3 %collective-permute-start.3 = (bf16[1,1,64,256]{3,2,1,0:T(8,128)(2,1)S(1)}, bf16[1,1,64,256]{3,2,1,0:T(8,128)(2,1)S(1)}, u32[]{:S(2)}, u32[]{:S(2)}) collective-permute-start(bf16[1,1,64,256]{3,2,1,0:T(8,128)(2,1)S(1)} %get-tuple-element.63), channel_id=1, source_target_pairs={{4,0},{8,4},{12,8},{5,1},{9,5},{13,9},{6,2},{10,6},{14,10},{7,3},{... | collective-permute-start | bytes 98312 | tf_op jit(solution)/shard_map/ppermute | solution.py:19
  73.4 4.5 %collective-permute-start.2 = (bf16[1,1,64,256]{3,2,1,0:T(8,128)(2,1)S(1)}, bf16[1,1,64,256]{3,2,1,0:T(8,128)(2,1)S(1)}, u32[]{:S(2)}, u32[]{:S(2)}) collective-permute-start(bf16[1,1,64,256]{3,2,1,0:T(8,128)(2,1)S(1)} %get-tuple-element.62), channel_id=1, source_target_pairs={{0,4},{4,8},{8,12},{1,5},{5,9},{9,13},{2,6},{6,10},{10,14},{3,7},{... | collective-permute-start | bytes 98312 | tf_op jit(solution)/shard_map/ppermute | solution.py:16
  77.9 0.8 multiply_convert_fusion
  78.8 1.3 %collective-permute-start.7 = (bf16[1,1,64,256]{3,2,1,0:T(8,128)(2,1)S(1)}, bf16[1,1,64,256]{3,2,1,0:T(8,128)(2,1)S(1)}, u32[]{:S(2)}, u32[]{:S(2)}) collective-permute-start(bf16[1,1,64,256]{3,2,1,0:T(8,128)(2,1)S(1)} %get-tuple-element.59), channel_id=1, source_target_pairs={{4,0},{8,4},{12,8},{5,1},{9,5},{13,9},{6,2},{10,6},{14,10},{7,3},{... | collective-permute-start | bytes 98312 | tf_op jit(solution)/shard_map/ppermute | solution.py:19
  80.1 4.5 %collective-permute-start.6 = (bf16[1,1,64,256]{3,2,1,0:T(8,128)(2,1)S(1)}, bf16[1,1,64,256]{3,2,1,0:T(8,128)(2,1)S(1)}, u32[]{:S(2)}, u32[]{:S(2)}) collective-permute-start(bf16[1,1,64,256]{3,2,1,0:T(8,128)(2,1)S(1)} %get-tuple-element.58), channel_id=1, source_target_pairs={{0,4},{4,8},{8,12},{1,5},{5,9},{9,13},{2,6},{6,10},{10,14},{3,7},{... | collective-permute-start | bytes 98312 | tf_op jit(solution)/shard_map/ppermute | solution.py:16
  84.6 5.7 %psum.87 = bf16[512]{0:T(512)(128)(2,1)S(1)} all-reduce(bf16[512]{0:T(512)(128)(2,1)S(1)} %convert_element_type.135), channel_id=1, replica_groups=mesh['groups'=2,'tile'=4,'image'=4] {'image'}, use_global_device_ids=true, to_apply=%region_26.27 | all-reduce | flops 512 | bytes 2048 | tf_op jit(solution)/shard_map/psum | solution.py:176
  90.3 0.6 convert_element_type.136
  91.1 0.9 fusion.47
  92.1 0.1 fusion.45
  92.2 0.3 fusion.61
  92.6 0.3 convolution_add_fusion.1
  92.9 0.3 convolution_add_fusion
  93.1 0.3 copy-done.5
  93.4 0.2 fusion.37
  93.7 0.1 reduce_sum.186
  93.9 0.1 reduce_sum.183
  94.0 10.2 %all-reduce.4 = (f32[1,32]{1,0:T(1,128)S(1)}, f32[1,32]{1,0:T(1,128)S(1)}) all-reduce(f32[1,32]{1,0:T(1,128)S(1)} %bitcast.138, f32[1,32]{1,0:T(1,128)S(1)} %bitcast.140), channel_id=1, replica_groups=mesh['groups'=2,'tile'=4,'image'=4] {'tile'}, use_global_device_ids=true, to_apply=%region_24.25 | all-reduce | flops 64 | bytes 512 | tf_op jit(solution)/shard_map/psum | solution.py:88
  104.6 0.3 fusion.59
  104.9 0.3 convolution_add_fusion.5
  105.2 0.9 fusion.2
  106.1 0.7 fusion.23
  106.9 9.7 %all-reduce.10.cloned.1.call-done = bf16[256,512]{1,0:T(8,128)(2,1)} async-done(((bf16[256,512]{1,0:T(8,128)(2,1)}), bf16[256,512]{1,0:T(8,128)(2,1)}) %all-reduce.10.cloned.1.call-update) | async-done | bytes 262160 | tf_op jit(solution)/shard_map/psum | solution.py:175
  116.6 1.8 %convert_element_type.134 = f32[256,512]{1,0:T(8,128)} convert(bf16[256,512]{1,0:T(8,128)(2,1)} %all-reduce.10.cloned.1.call-done) | non-fusion elementwise | flops 131072 | bytes 786432 | tf_op jit(solution)/shard_map/convert_element_type | solution.py:175
  (102 shorter events, 3.2 us)
Async XLA Ops:
  7.2 37.4 %copy-start = (bf16[1000,256]{1,0:T(8,128)(2,1)S(1)}, bf16[1000,256]{1,0:T(8,128)(2,1)}, u32[]{:S(2)}) copy-start(bf16[1000,256]{1,0:T(8,128)(2,1)} %param.23) | copy-start | bytes 1536004
  7.2 109.4 %all-reduce.10.cloned.1.call-start = ((), (), s32[]{:S(2)}) async-start(), calls=%async_computation | async-start | bytes 524288 | tf_op jit(solution)/shard_map/psum | solution.py:175
  24.1 21.6 %collective-permute-start.1 = (bf16[1,1,64,256]{3,2,1,0:T(8,128)(2,1)}, bf16[1,1,64,256]{3,2,1,0:T(8,128)(2,1)S(1)}, u32[]{:S(2)}, u32[]{:S(2)}) collective-permute-start(bf16[1,1,64,256]{3,2,1,0:T(8,128)(2,1)} %get-tuple-element.65), channel_id=1, source_target_pairs={{4,0},{8,4},{12,8},{5,1},{9,5},{13,9},{6,2},{10,6},{14,10},{7,3},{... | collective-permute-start | bytes 98312 | tf_op jit(solution)/shard_map/ppermute | solution.py:19
  25.4 20.4 %collective-permute-start = (bf16[1,1,64,256]{3,2,1,0:T(8,128)(2,1)}, bf16[1,1,64,256]{3,2,1,0:T(8,128)(2,1)S(1)}, u32[]{:S(2)}, u32[]{:S(2)}) collective-permute-start(bf16[1,1,64,256]{3,2,1,0:T(8,128)(2,1)} %get-tuple-element.64), channel_id=1, source_target_pairs={{0,4},{4,8},{8,12},{1,5},{5,9},{9,13},{2,6},{6,10},{10,14},{3,7},{... | collective-permute-start | bytes 98312 | tf_op jit(solution)/shard_map/ppermute | solution.py:16
  31.4 28.4 %collective-permute-start.4 = (bf16[1,1,64,256]{3,2,1,0:T(8,128)(2,1)}, bf16[1,1,64,256]{3,2,1,0:T(8,128)(2,1)S(1)}, u32[]{:S(2)}, u32[]{:S(2)}) collective-permute-start(bf16[1,1,64,256]{3,2,1,0:T(8,128)(2,1)} %get-tuple-element.61), channel_id=1, source_target_pairs={{0,4},{4,8},{8,12},{1,5},{5,9},{9,13},{2,6},{6,10},{10,14},{3,7},{... | collective-permute-start | bytes 98312 | tf_op jit(solution)/shard_map/ppermute | solution.py:16
  33.3 3.8 %copy-start.1 = (bf16[3,3,256,256]{3,2,1,0:T(8,128)(2,1)S(1)}, bf16[3,3,256,256]{3,2,1,0:T(8,128)(2,1)}, u32[]{:S(2)}) copy-start(bf16[3,3,256,256]{3,2,1,0:T(8,128)(2,1)} %param.20) | copy-start | bytes 3538948
  33.3 26.8 %collective-permute-start.5 = (bf16[1,1,64,256]{3,2,1,0:T(8,128)(2,1)}, bf16[1,1,64,256]{3,2,1,0:T(8,128)(2,1)S(1)}, u32[]{:S(2)}, u32[]{:S(2)}) collective-permute-start(bf16[1,1,64,256]{3,2,1,0:T(8,128)(2,1)} %get-tuple-element.60), channel_id=1, source_target_pairs={{4,0},{8,4},{12,8},{5,1},{9,5},{13,9},{6,2},{10,6},{14,10},{7,3},{... | collective-permute-start | bytes 98312 | tf_op jit(solution)/shard_map/ppermute | solution.py:19
  37.1 1.6 %copy-start.2 = (bf16[3,3,256,256]{3,2,1,0:T(8,128)(2,1)S(1)}, bf16[3,3,256,256]{3,2,1,0:T(8,128)(2,1)}, u32[]{:S(2)}) copy-start(bf16[3,3,256,256]{3,2,1,0:T(8,128)(2,1)} %param.19) | copy-start | bytes 3538948
  39.7 3.0 %copy-start.3 = (bf16[3,3,256,256]{2,3,1,0:T(8,128)(2,1)S(1)}, bf16[3,3,256,256]{2,3,1,0:T(8,128)(2,1)}, u32[]{:S(2)}) copy-start(bf16[3,3,256,256]{2,3,1,0:T(8,128)(2,1)} %copy.17) | copy-start | bytes 3538948
  42.8 1.6 %copy-start.4 = (bf16[3,3,256,256]{2,3,1,0:T(8,128)(2,1)S(1)}, bf16[3,3,256,256]{2,3,1,0:T(8,128)(2,1)}, u32[]{:S(2)}) copy-start(bf16[3,3,256,256]{2,3,1,0:T(8,128)(2,1)} %copy.18) | copy-start | bytes 3538948
  44.4 0.9 copy-start.16
  44.4 1.0 copy-start.20
  44.5 1.1 copy-start.15
  46.0 1.0 copy-start.12
  46.0 1.3 %copy-start.11 = (bf16[1,3,256,256]{3,2,1,0:T(8,128)(2,1)S(1)}, bf16[1,3,256,256]{3,2,1,0:T(8,128)(2,1)}, u32[]{:S(2)}) copy-start(bf16[1,3,256,256]{3,2,1,0:T(8,128)(2,1)} %get-tuple-element.34) | copy-start | bytes 1179652
  47.0 1.0 copy-start.10
  47.3 12.5 %copy-start.19 = (f32[512]{0:T(512)S(1)}, f32[512]{0:T(512)}, u32[]{:S(2)}) copy-start(f32[512]{0:T(512)} %param.25) | copy-start | bytes 6148
  47.3 12.5 %copy-start.14 = (bf16[1,4,64,256]{3,2,1,0:T(8,128)(2,1)S(1)}, bf16[1,4,64,256]{3,2,1,0:T(8,128)(2,1)}, u32[]{:S(2)}) copy-start(bf16[1,4,64,256]{3,2,1,0:T(8,128)(2,1)} %param.14) | copy-start | bytes 393220
  60.3 1.0 copy-start.8
  61.3 1.0 copy-start.13
  72.1 18.8 %collective-permute-start.3 = (bf16[1,1,64,256]{3,2,1,0:T(8,128)(2,1)S(1)}, bf16[1,1,64,256]{3,2,1,0:T(8,128)(2,1)S(1)}, u32[]{:S(2)}, u32[]{:S(2)}) collective-permute-start(bf16[1,1,64,256]{3,2,1,0:T(8,128)(2,1)S(1)} %get-tuple-element.63), channel_id=1, source_target_pairs={{4,0},{8,4},{12,8},{5,1},{9,5},{13,9},{6,2},{10,6},{14,10},{7,3},{... | collective-permute-start | bytes 98312 | tf_op jit(solution)/shard_map/ppermute | solution.py:19
  73.4 17.5 %collective-permute-start.2 = (bf16[1,1,64,256]{3,2,1,0:T(8,128)(2,1)S(1)}, bf16[1,1,64,256]{3,2,1,0:T(8,128)(2,1)S(1)}, u32[]{:S(2)}, u32[]{:S(2)}) collective-permute-start(bf16[1,1,64,256]{3,2,1,0:T(8,128)(2,1)S(1)} %get-tuple-element.62), channel_id=1, source_target_pairs={{0,4},{4,8},{8,12},{1,5},{5,9},{9,13},{2,6},{6,10},{10,14},{3,7},{... | collective-permute-start | bytes 98312 | tf_op jit(solution)/shard_map/ppermute | solution.py:16
  78.8 13.2 %collective-permute-start.7 = (bf16[1,1,64,256]{3,2,1,0:T(8,128)(2,1)S(1)}, bf16[1,1,64,256]{3,2,1,0:T(8,128)(2,1)S(1)}, u32[]{:S(2)}, u32[]{:S(2)}) collective-permute-start(bf16[1,1,64,256]{3,2,1,0:T(8,128)(2,1)S(1)} %get-tuple-element.59), channel_id=1, source_target_pairs={{4,0},{8,4},{12,8},{5,1},{9,5},{13,9},{6,2},{10,6},{14,10},{7,3},{... | collective-permute-start | bytes 98312 | tf_op jit(solution)/shard_map/ppermute | solution.py:19
  80.1 11.9 %collective-permute-start.6 = (bf16[1,1,64,256]{3,2,1,0:T(8,128)(2,1)S(1)}, bf16[1,1,64,256]{3,2,1,0:T(8,128)(2,1)S(1)}, u32[]{:S(2)}, u32[]{:S(2)}) collective-permute-start(bf16[1,1,64,256]{3,2,1,0:T(8,128)(2,1)S(1)} %get-tuple-element.58), channel_id=1, source_target_pairs={{0,4},{4,8},{8,12},{1,5},{5,9},{9,13},{2,6},{6,10},{10,14},{3,7},{... | collective-permute-start | bytes 98312 | tf_op jit(solution)/shard_map/ppermute | solution.py:16
  92.5 0.9 copy-start.5
  92.5 0.9 copy-start.17
  92.5 0.9 copy-start.18
  92.8 11.8 %copy-start.7 = (bf16[1,3,256,256]{3,2,1,0:T(8,128)(2,1)S(1)}, bf16[1,3,256,256]{3,2,1,0:T(8,128)(2,1)}, u32[]{:S(2)}) copy-start(bf16[1,3,256,256]{3,2,1,0:T(8,128)(2,1)} %get-tuple-element.32) | copy-start | bytes 1179652
  92.8 11.8 %copy-start.9 = (bf16[1,4,64,768]{3,2,1,0:T(8,128)(2,1)S(1)}, bf16[1,4,64,768]{3,2,1,0:T(8,128)(2,1)}, u32[]{:S(2)}) copy-start(bf16[1,4,64,768]{3,2,1,0:T(8,128)(2,1)} %get-tuple-element.44) | copy-start | bytes 1179652
  93.4 11.5 %copy-start.6 = (bf16[1,3,256,256]{3,2,1,0:T(8,128)(2,1)S(1)}, bf16[1,3,256,256]{3,2,1,0:T(8,128)(2,1)}, u32[]{:S(2)}) copy-start(bf16[1,3,256,256]{3,2,1,0:T(8,128)(2,1)} %get-tuple-element.31) | copy-start | bytes 1179652
Sparse Core Ops, SparseCore 0:
  84.8 31.7 all-reduce.9
where the time goes:
time: 126 us; the launch traced here: 125 us
  blocking collectives  48.9 us (39%)
  starting transfers between devices  20.9 us (17%)
  local copies, waits for them, and re-layouts  17.4 us (14%)
  between operations  16 us (13%)
  waiting for transfers between devices  9.77 us (8%)
  other arithmetic  7.85 us (6%)
  matrix products  4.46 us (4%)
    ppermute x4, starting transfers between devices, with_halo(): lax.ppermute(lax.slice_in_dim(block, block.shape[dim] - width, None, axis...  15.6 us
    psum x1, blocking collectives, moments(): first_sum, square_sum = lax.psum((first_sum, square_sum), 'tile')  13.5 us
    psum x1, blocking collectives, body(): modulation = lax.psum(partial_terms, 'tile') + adaptive_bias  11 us
    psum x1, blocking collectives, norm_back_first(): plain_sum, paired_sum = lax.psum((plain_sum, paired_sum), 'tile')  10.2 us
    psum x1, waiting for transfers between devices, body(): lax.psum(local_weight.astype(jnp.bfloat16), 'image').astype(jnp.float32)  9.73 us
    unnamed x46, local copies, waits for them, and re-layouts  8.78 us
    psum x1, blocking collectives, body(): scale_sum, shift_sum = lax.psum((scale_sum, shift_sum), 'tile')  8.47 us
    psum x1, blocking collectives, body(): lax.psum(local_bias.astype(jnp.bfloat16), 'image').astype(jnp.float32)  5.67 us
  transfers between devices with their start and end apart: 9, of which 1 were waited for; matrix products, arithmetic and copies ran while one was open for 14% of the time, Pallas kernels for 0%

commit v1 on v0

--- a/solution.py
+++ b/solution.py
@@ -108,6 +108,12 @@
     adaptive_weight,
     adaptive_bias,
 ):
+
+    def handle_area(piece_in):
+        value_now = lax.all_gather(piece_in, "tile")
+        o_now = jnp.sum(value_now, axis=0)
+        return o_now
+
     channels = images.shape[3]
     half_freq = time_weight.shape[0] // 2
     frequencies = jnp.exp(-math.log(10000.0) * jnp.arange(half_freq, dtype=jnp.float32) / half_freq)
@@ -127,7 +133,7 @@
     partial_terms = jnp.dot(
         activated, adaptive_weight.astype(jnp.float32), precision=lax.Precision.HIGHEST
     )
-    modulation = lax.psum(partial_terms, "tile") + adaptive_bias
+    modulation = handle_area(partial_terms) + adaptive_bias
     factor_row = 1.0 + modulation[:, :channels]
     factor = factor_row[:, None, None, :]
     shift_term = modulation[:, channels:][:, None, None, :]

time: 126 us -> 139 us (1.10)
  blocking collectives: 48.9 us -> 59.9 us
  matrix products: 4.46 us -> 6.33 us
    all_gather x0 -> x1, blocking collectives: none -> 11.9 us  [handle_area(): value_now = lax.all_gather(piece_in, 'tile')]
    psum x1 -> x0, blocking collectives: 11 us -> none  [body(): modulation = lax.psum(partial_terms, 'tile') + adaptive_bias]
    psum x1 -> x2, blocking collectives: 13.5 us -> 23.6 us  [moments(): first_sum, square_sum = lax.psum((first_sum, square_sum), 'tile')]
    unnamed x46 -> x42, local copies, waits for them, and re-layouts: 8.78 us -> 8.76 us
where the time goes in v1:
time: 139 us; the launch traced here: 138 us
  blocking collectives  59.9 us (43%)
  starting transfers between devices  20.9 us (15%)
  local copies, waits for them, and re-layouts  17.4 us (13%)
  between operations  15.9 us (11%)
  waiting for transfers between devices  9.77 us (7%)
  other arithmetic  7.87 us (6%)
  matrix products  6.33 us (5%)
    psum x2, blocking collectives, moments(): first_sum, square_sum = lax.psum((first_sum, square_sum), 'tile')  23.6 us
    ppermute x4, starting transfers between devices, with_halo(): lax.ppermute(lax.slice_in_dim(block, block.shape[dim] - width, None, axis...  15.6 us
    all_gather x1, blocking collectives, handle_area(): value_now = lax.all_gather(piece_in, 'tile')  11.9 us
    psum x1, blocking collectives, norm_back_first(): plain_sum, paired_sum = lax.psum((plain_sum, paired_sum), 'tile')  10.1 us
    psum x1, waiting for transfers between devices, body(): lax.psum(local_weight.astype(jnp.bfloat16), 'image').astype(jnp.float32)  9.73 us
    unnamed x42, local copies, waits for them, and re-layouts  8.76 us
    psum x1, blocking collectives, body(): scale_sum, shift_sum = lax.psum((scale_sum, shift_sum), 'tile')  8.66 us
    psum x1, blocking collectives, body(): lax.psum(local_bias.astype(jnp.bfloat16), 'image').astype(jnp.float32)  5.67 us
  transfers between devices with their start and end apart: 9, of which 1 were waited for; matrix products, arithmetic and copies ran while one was open for 14% of the time, Pallas kernels for 0%

profile of v1, /device:TPU:0, one launch (start us, length us, event | category | flops | bytes accessed | tf_op | source)
XLA Modules:
  0.0 138.1 jit_solution(15355980808841798515)
XLA Ops:
  7.2 1.0 convert_reduce_fusion
  8.4 0.1 reduce_sum.177
  8.5 0.1 reduce_sum.174
  8.6 13.5 %all-reduce.7 = (f32[1,32]{1,0:T(1,128)S(1)}, f32[1,32]{1,0:T(1,128)S(1)}) all-reduce(f32[1,32]{1,0:T(1,128)S(1)} %bitcast.142, f32[1,32]{1,0:T(1,128)S(1)} %bitcast.144), channel_id=1, replica_groups=mesh['groups'=2,'tile'=4,'image'=4] {'tile'}, use_global_device_ids=true, to_apply=%region_5.6 | all-reduce | flops 64 | bytes 512 | tf_op jit(solution)/shard_map/psum | solution.py:66
  22.5 1.0 fusion.15
  23.5 0.6 fusion.55
  24.1 1.3 collective-permute-start.1
  25.4 4.5 %collective-permute-start = (bf16[1,1,64,256]{3,2,1,0:T(8,128)(2,1)}, bf16[1,1,64,256]{3,2,1,0:T(8,128)(2,1)S(1)}, u32[]{:S(2)}, u32[]{:S(2)}) collective-permute-start(bf16[1,1,64,256]{3,2,1,0:T(8,128)(2,1)} %get-tuple-element.63), channel_id=1, source_target_pairs={{0,4},{4,8},{8,12},{1,5},{5,9},{9,13},{2,6},{6,10},{10,14},{3,7},{... | collective-permute-start | bytes 98312 | tf_op jit(solution)/shard_map/ppermute | solution.py:16
  30.0 1.4 %fusion.53 = (bf16[1,1,64,256]{3,2,1,0:T(8,128)(2,1)}, bf16[1,1,64,256]{3,2,1,0:T(8,128)(2,1)}) fusion(bf16[1,4,64,256]{3,2,1,0:T(8,128)(2,1)} %param.14), kind=kLoop, calls=%fused_computation.108 | loop fusion | bytes 131072 | tf_op jit(solution)/shard_map/slice | solution.py:19
  31.4 1.9 %collective-permute-start.4 = (bf16[1,1,64,256]{3,2,1,0:T(8,128)(2,1)}, bf16[1,1,64,256]{3,2,1,0:T(8,128)(2,1)S(1)}, u32[]{:S(2)}, u32[]{:S(2)}) collective-permute-start(bf16[1,1,64,256]{3,2,1,0:T(8,128)(2,1)} %get-tuple-element.60), channel_id=1, source_target_pairs={{0,4},{4,8},{8,12},{1,5},{5,9},{9,13},{2,6},{6,10},{10,14},{3,7},{... | collective-permute-start | bytes 98312 | tf_op jit(solution)/shard_map/ppermute | solution.py:16
  33.3 1.4 %collective-permute-start.5 = (bf16[1,1,64,256]{3,2,1,0:T(8,128)(2,1)}, bf16[1,1,64,256]{3,2,1,0:T(8,128)(2,1)S(1)}, u32[]{:S(2)}, u32[]{:S(2)}) collective-permute-start(bf16[1,1,64,256]{3,2,1,0:T(8,128)(2,1)} %get-tuple-element.59), channel_id=1, source_target_pairs={{4,0},{8,4},{12,8},{5,1},{9,5},{13,9},{6,2},{10,6},{14,10},{7,3},{... | collective-permute-start | bytes 98312 | tf_op jit(solution)/shard_map/ppermute | solution.py:19
  34.7 2.4 %copy.19 = bf16[3,3,256,256]{2,3,1,0:T(8,128)(2,1)} copy(bf16[3,3,256,256]{3,2,1,0:T(8,128)(2,1)} %param.20) | data formatting | bytes 2359296 | tf_op args[7]
  37.1 1.0 fusion.43
  38.1 0.6 copy-done.2
  38.7 1.0 fusion.44
  39.7 1.6 %copy.20 = bf16[3,3,256,256]{2,3,1,0:T(8,128)(2,1)} copy(bf16[3,3,256,256]{3,2,1,0:T(8,128)(2,1)S(1)} %copy-done.2) | data formatting | bytes 2359296 | tf_op args[6]
  42.7 0.2 fusion.57
  42.9 1.0 fusion.31
  44.0 1.2 convolution_bitcast_fusion
  45.2 11.9 %all-gather.1 = f32[4,1,512]{2,1,0:T(1,128)S(1)} all-gather(f32[1,1,512]{2,1,0:T(1,128)S(1)} %convolution_bitcast_fusion), channel_id=2, replica_groups=mesh['groups'=2,'tile'=4,'image'=4] {'tile'}, dimensions={0}, use_global_device_ids=true | all-gather | bytes 10240 | tf_op jit(solution)/shard_map/all_gather | solution.py:113
  57.2 1.0 fusion.42
  58.2 0.6 copy-done.4
  59.0 0.6 copy-done.17
  59.9 0.9 copy-done.12
  60.8 0.3 fusion.56
  61.1 0.3 convolution_add_fusion.7
  61.3 0.5 copy-done.9
  61.8 0.3 fusion.39
  62.2 0.1 reduce_sum.183
  62.4 0.1 reduce_sum.180
  62.5 10.1 %all-reduce.6 = (f32[1,32]{1,0:T(1,128)S(1)}, f32[1,32]{1,0:T(1,128)S(1)}) all-reduce(f32[1,32]{1,0:T(1,128)S(1)} %bitcast.141, f32[1,32]{1,0:T(1,128)S(1)} %bitcast.145), channel_id=1, replica_groups=mesh['groups'=2,'tile'=4,'image'=4] {'tile'}, use_global_device_ids=true, to_apply=%region_11.12 | all-reduce | flops 64 | bytes 512 | tf_op jit(solution)/shard_map/psum | solution.py:66
  73.1 0.1 fusion.46
  73.3 0.9 copy-done.8
  74.1 0.3 fusion.59
  74.4 0.3 convolution_add_fusion.3
  74.7 0.4 copy-done.13
  75.1 0.3 fusion.38
  75.4 8.7 %all-reduce.5 = (f32[1,256]{1,0:T(1,128)S(1)}, f32[1,256]{1,0:T(1,128)S(1)}) all-reduce(f32[1,256]{1,0:T(1,128)S(1)} %bitcast.138, f32[1,256]{1,0:T(1,128)S(1)} %bitcast.139), channel_id=1, replica_groups=mesh['groups'=2,'tile'=4,'image'=4] {'tile'}, use_global_device_ids=true, to_apply=%region_14.15 | all-reduce | flops 512 | bytes 4096 | tf_op jit(solution)/shard_map/psum | solution.py:159
  84.2 0.1 reduce_sum.191
  84.6 0.1 reduce_sum.188
  84.9 0.2 multiply_convert_fusion.1
  85.1 1.3 collective-permute-start.3
  86.4 4.5 %collective-permute-start.2 = (bf16[1,1,64,256]{3,2,1,0:T(8,128)(2,1)S(1)}, bf16[1,1,64,256]{3,2,1,0:T(8,128)(2,1)S(1)}, u32[]{:S(2)}, u32[]{:S(2)}) collective-permute-start(bf16[1,1,64,256]{3,2,1,0:T(8,128)(2,1)S(1)} %get-tuple-element.61), channel_id=1, source_target_pairs={{0,4},{4,8},{8,12},{1,5},{5,9},{9,13},{2,6},{6,10},{10,14},{3,7},{... | collective-permute-start | bytes 98312 | tf_op jit(solution)/shard_map/ppermute | solution.py:16
  91.0 0.8 multiply_convert_fusion
  91.8 1.3 collective-permute-start.7
  93.1 4.5 %collective-permute-start.6 = (bf16[1,1,64,256]{3,2,1,0:T(8,128)(2,1)S(1)}, bf16[1,1,64,256]{3,2,1,0:T(8,128)(2,1)S(1)}, u32[]{:S(2)}, u32[]{:S(2)}) collective-permute-start(bf16[1,1,64,256]{3,2,1,0:T(8,128)(2,1)S(1)} %get-tuple-element.57), channel_id=1, source_target_pairs={{0,4},{4,8},{8,12},{1,5},{5,9},{9,13},{2,6},{6,10},{10,14},{3,7},{... | collective-permute-start | bytes 98312 | tf_op jit(solution)/shard_map/ppermute | solution.py:16
  97.7 5.7 %psum.79 = bf16[512]{0:T(512)(128)(2,1)S(1)} all-reduce(bf16[512]{0:T(512)(128)(2,1)S(1)} %convert_element_type.135), channel_id=1, replica_groups=mesh['groups'=2,'tile'=4,'image'=4] {'image'}, use_global_device_ids=true, to_apply=%region_26.27 | all-reduce | flops 512 | bytes 2048 | tf_op jit(solution)/shard_map/psum | solution.py:182
  103.3 0.6 convert_element_type.136
  104.1 0.9 fusion.47
  105.2 0.1 fusion.45
  105.3 0.3 fusion.60
  105.6 0.3 convolution_add_fusion.1
  105.9 0.3 convolution_add_fusion
  106.2 0.3 copy-done.5
  106.5 0.2 fusion.37
  106.7 0.1 reduce_sum.196
  106.9 0.1 reduce_sum.193
  107.1 10.1 %all-reduce.4 = (f32[1,32]{1,0:T(1,128)S(1)}, f32[1,32]{1,0:T(1,128)S(1)}) all-reduce(f32[1,32]{1,0:T(1,128)S(1)} %bitcast.140, f32[1,32]{1,0:T(1,128)S(1)} %bitcast.143), channel_id=1, replica_groups=mesh['groups'=2,'tile'=4,'image'=4] {'tile'}, use_global_device_ids=true, to_apply=%region_24.25 | all-reduce | flops 64 | bytes 512 | tf_op jit(solution)/shard_map/psum | solution.py:88
  117.5 0.3 fusion.58
  117.8 0.3 convolution_add_fusion.5
  118.0 0.9 fusion.2
  119.0 0.7 fusion.23
  119.7 9.7 %all-reduce.10.cloned.1.call-done = bf16[256,512]{1,0:T(8,128)(2,1)} async-done(((bf16[256,512]{1,0:T(8,128)(2,1)}), bf16[256,512]{1,0:T(8,128)(2,1)}) %all-reduce.10.cloned.1.call-update) | async-done | bytes 262160 | tf_op jit(solution)/shard_map/psum | solution.py:181
  129.4 1.8 %convert_element_type.134 = f32[256,512]{1,0:T(8,128)} convert(bf16[256,512]{1,0:T(8,128)(2,1)} %all-reduce.10.cloned.1.call-done) | non-fusion elementwise | flops 131072 | bytes 786432 | tf_op jit(solution)/shard_map/convert_element_type | solution.py:181
  (100 shorter events, 3.3 us)
Async XLA Ops:
  7.2 35.5 %copy-start = (bf16[1000,256]{1,0:T(8,128)(2,1)S(1)}, bf16[1000,256]{1,0:T(8,128)(2,1)}, u32[]{:S(2)}) copy-start(bf16[1000,256]{1,0:T(8,128)(2,1)} %param.23) | copy-start | bytes 1536004
  7.2 122.3 %all-reduce.10.cloned.1.call-start = ((), (), s32[]{:S(2)}) async-start(), calls=%async_computation | async-start | bytes 524288 | tf_op jit(solution)/shard_map/psum | solution.py:181
  24.1 35.4 %collective-permute-start.1 = (bf16[1,1,64,256]{3,2,1,0:T(8,128)(2,1)}, bf16[1,1,64,256]{3,2,1,0:T(8,128)(2,1)S(1)}, u32[]{:S(2)}, u32[]{:S(2)}) collective-permute-start(bf16[1,1,64,256]{3,2,1,0:T(8,128)(2,1)} %get-tuple-element.64), channel_id=1, source_target_pairs={{4,0},{8,4},{12,8},{5,1},{9,5},{13,9},{6,2},{10,6},{14,10},{7,3},{... | collective-permute-start | bytes 98312 | tf_op jit(solution)/shard_map/ppermute | solution.py:19
  25.4 34.1 %collective-permute-start = (bf16[1,1,64,256]{3,2,1,0:T(8,128)(2,1)}, bf16[1,1,64,256]{3,2,1,0:T(8,128)(2,1)S(1)}, u32[]{:S(2)}, u32[]{:S(2)}) collective-permute-start(bf16[1,1,64,256]{3,2,1,0:T(8,128)(2,1)} %get-tuple-element.63), channel_id=1, source_target_pairs={{0,4},{4,8},{8,12},{1,5},{5,9},{9,13},{2,6},{6,10},{10,14},{3,7},{... | collective-permute-start | bytes 98312 | tf_op jit(solution)/shard_map/ppermute | solution.py:16
  31.4 41.2 %collective-permute-start.4 = (bf16[1,1,64,256]{3,2,1,0:T(8,128)(2,1)}, bf16[1,1,64,256]{3,2,1,0:T(8,128)(2,1)S(1)}, u32[]{:S(2)}, u32[]{:S(2)}) collective-permute-start(bf16[1,1,64,256]{3,2,1,0:T(8,128)(2,1)} %get-tuple-element.60), channel_id=1, source_target_pairs={{0,4},{4,8},{8,12},{1,5},{5,9},{9,13},{2,6},{6,10},{10,14},{3,7},{... | collective-permute-start | bytes 98312 | tf_op jit(solution)/shard_map/ppermute | solution.py:16
  33.3 3.8 %copy-start.1 = (bf16[3,3,256,256]{3,2,1,0:T(8,128)(2,1)S(1)}, bf16[3,3,256,256]{3,2,1,0:T(8,128)(2,1)}, u32[]{:S(2)}) copy-start(bf16[3,3,256,256]{3,2,1,0:T(8,128)(2,1)} %param.20) | copy-start | bytes 3538948
  33.3 39.7 %collective-permute-start.5 = (bf16[1,1,64,256]{3,2,1,0:T(8,128)(2,1)}, bf16[1,1,64,256]{3,2,1,0:T(8,128)(2,1)S(1)}, u32[]{:S(2)}, u32[]{:S(2)}) collective-permute-start(bf16[1,1,64,256]{3,2,1,0:T(8,128)(2,1)} %get-tuple-element.59), channel_id=1, source_target_pairs={{4,0},{8,4},{12,8},{5,1},{9,5},{13,9},{6,2},{10,6},{14,10},{7,3},{... | collective-permute-start | bytes 98312 | tf_op jit(solution)/shard_map/ppermute | solution.py:19
  37.1 1.6 %copy-start.2 = (bf16[3,3,256,256]{3,2,1,0:T(8,128)(2,1)S(1)}, bf16[3,3,256,256]{3,2,1,0:T(8,128)(2,1)}, u32[]{:S(2)}) copy-start(bf16[3,3,256,256]{3,2,1,0:T(8,128)(2,1)} %param.19) | copy-start | bytes 3538948
  39.7 4.2 %copy-start.18 = (f32[256]{0:T(256)S(1)}, f32[256]{0:T(256)}, u32[]{:S(2)}) copy-start(f32[256]{0:T(256)} %param.22) | copy-start | bytes 3076
  39.7 17.4 %copy-start.3 = (bf16[3,3,256,256]{2,3,1,0:T(8,128)(2,1)S(1)}, bf16[3,3,256,256]{2,3,1,0:T(8,128)(2,1)}, u32[]{:S(2)}) copy-start(bf16[3,3,256,256]{2,3,1,0:T(8,128)(2,1)} %copy.19) | copy-start | bytes 3538948
  57.2 1.6 %copy-start.4 = (bf16[3,3,256,256]{2,3,1,0:T(8,128)(2,1)S(1)}, bf16[3,3,256,256]{2,3,1,0:T(8,128)(2,1)}, u32[]{:S(2)}) copy-start(bf16[3,3,256,256]{2,3,1,0:T(8,128)(2,1)} %copy.20) | copy-start | bytes 3538948
  58.9 0.7 copy-start.17
  59.8 1.0 copy-start.12
  59.8 1.3 copy-start.10
  60.8 1.0 copy-start.9
  61.0 11.6 %copy-start.14 = (bf16[1,4,64,256]{3,2,1,0:T(8,128)(2,1)S(1)}, bf16[1,4,64,256]{3,2,1,0:T(8,128)(2,1)}, u32[]{:S(2)}) copy-start(bf16[1,4,64,256]{3,2,1,0:T(8,128)(2,1)} %param.14) | copy-start | bytes 393220
  73.1 1.0 copy-start.8
  74.1 1.0 copy-start.13
  85.1 18.8 %collective-permute-start.3 = (bf16[1,1,64,256]{3,2,1,0:T(8,128)(2,1)S(1)}, bf16[1,1,64,256]{3,2,1,0:T(8,128)(2,1)S(1)}, u32[]{:S(2)}, u32[]{:S(2)}) collective-permute-start(bf16[1,1,64,256]{3,2,1,0:T(8,128)(2,1)S(1)} %get-tuple-element.62), channel_id=1, source_target_pairs={{4,0},{8,4},{12,8},{5,1},{9,5},{13,9},{6,2},{10,6},{14,10},{7,3},{... | collective-permute-start | bytes 98312 | tf_op jit(solution)/shard_map/ppermute | solution.py:19
  86.4 17.5 %collective-permute-start.2 = (bf16[1,1,64,256]{3,2,1,0:T(8,128)(2,1)S(1)}, bf16[1,1,64,256]{3,2,1,0:T(8,128)(2,1)S(1)}, u32[]{:S(2)}, u32[]{:S(2)}) collective-permute-start(bf16[1,1,64,256]{3,2,1,0:T(8,128)(2,1)S(1)} %get-tuple-element.61), channel_id=1, source_target_pairs={{0,4},{4,8},{8,12},{1,5},{5,9},{9,13},{2,6},{6,10},{10,14},{3,7},{... | collective-permute-start | bytes 98312 | tf_op jit(solution)/shard_map/ppermute | solution.py:16
  91.8 13.2 %collective-permute-start.7 = (bf16[1,1,64,256]{3,2,1,0:T(8,128)(2,1)S(1)}, bf16[1,1,64,256]{3,2,1,0:T(8,128)(2,1)S(1)}, u32[]{:S(2)}, u32[]{:S(2)}) collective-permute-start(bf16[1,1,64,256]{3,2,1,0:T(8,128)(2,1)S(1)} %get-tuple-element.58), channel_id=1, source_target_pairs={{4,0},{8,4},{12,8},{5,1},{9,5},{13,9},{6,2},{10,6},{14,10},{7,3},{... | collective-permute-start | bytes 98312 | tf_op jit(solution)/shard_map/ppermute | solution.py:19
  93.1 11.9 %collective-permute-start.6 = (bf16[1,1,64,256]{3,2,1,0:T(8,128)(2,1)S(1)}, bf16[1,1,64,256]{3,2,1,0:T(8,128)(2,1)S(1)}, u32[]{:S(2)}, u32[]{:S(2)}) collective-permute-start(bf16[1,1,64,256]{3,2,1,0:T(8,128)(2,1)S(1)} %get-tuple-element.57), channel_id=1, source_target_pairs={{0,4},{4,8},{8,12},{1,5},{5,9},{9,13},{2,6},{6,10},{10,14},{3,7},{... | collective-permute-start | bytes 98312 | tf_op jit(solution)/shard_map/ppermute | solution.py:16
  105.5 0.9 copy-start.5
  105.6 0.9 copy-start.15
  105.6 0.9 copy-start.16
  105.9 11.6 %copy-start.7 = (bf16[1,3,256,256]{3,2,1,0:T(8,128)(2,1)S(1)}, bf16[1,3,256,256]{3,2,1,0:T(8,128)(2,1)}, u32[]{:S(2)}) copy-start(bf16[1,3,256,256]{3,2,1,0:T(8,128)(2,1)} %get-tuple-element.31) | copy-start | bytes 1179652
  105.9 11.6 %copy-start.11 = (bf16[1,4,64,768]{3,2,1,0:T(8,128)(2,1)S(1)}, bf16[1,4,64,768]{3,2,1,0:T(8,128)(2,1)}, u32[]{:S(2)}) copy-start(bf16[1,4,64,768]{3,2,1,0:T(8,128)(2,1)} %get-tuple-element.43) | copy-start | bytes 1179652
  106.5 11.3 %copy-start.6 = (bf16[1,3,256,256]{3,2,1,0:T(8,128)(2,1)S(1)}, bf16[1,3,256,256]{3,2,1,0:T(8,128)(2,1)}, u32[]{:S(2)}) copy-start(bf16[1,3,256,256]{3,2,1,0:T(8,128)(2,1)} %get-tuple-element.30) | copy-start | bytes 1179652
Sparse Core Ops, SparseCore 0:
  97.8 31.5 all-reduce.9
